TPU v7x, 32 devices: a whole 2x2x4 slice. The times are simulated.
32 devices in a mesh: row: 8 (over z, x), col: 4 (over y, core).
Axes of the slice: x: 2, y: 2, z: 4, core: 2. Of those that a mesh axis runs over, the one named last changes fastest.
Arguments:
- affinity: bfloat16 [32768, 8192], P('row', 'col'), may hold values from -250 to 250
- seed_values: int32 [16], replicated, may hold values from 0 to 1073741823
- sku_ids: int32 [8192], P('col'), may hold values from 0 to 8191, each once
Outputs:
- range_basis: float32 [16, 32768], P(None, ('row', 'col'))
- range_factor: float32 [16, 16], replicated
All inputs are finite; a program needn't handle non-finite values.
Results may differ from a plain program's by a relative error of at most 0.0046.
Values may be sent and summed in bfloat16 or wider, within the bound.
A program may use at most 64 MiB of HBM per device.

v0:
```python
import math
import jax
import jax.numpy as jnp
from jax import lax
from jax.sharding import PartitionSpec as P

ITERS = 2
mix_first = -2048144789
mix_second = -1028477387
golden = -1640531535
salt_value = 1540483477


def shifted(value, amount):
    return lax.shift_right_logical(value, jnp.full(value.shape, amount, jnp.int32))


def scramble(value):
    value = jnp.bitwise_xor(value, shifted(value, 16))
    value = value * jnp.int32(mix_first)
    value = jnp.bitwise_xor(value, shifted(value, 13))
    value = value * jnp.int32(mix_second)
    return jnp.bitwise_xor(value, shifted(value, 16))


def test_matrix(seed_values, sku_ids, total_columns):
    first = scramble(jnp.bitwise_xor(seed_values[:, None], sku_ids[None, :] * jnp.int32(golden)))
    second = scramble(jnp.bitwise_xor(first, jnp.int32(salt_value)))
    uniform_a = (shifted(first, 9) + 1).astype(jnp.float32) / 8388608.0
    uniform_b = (shifted(second, 9) + 1).astype(jnp.float32) / 8388608.0
    gauss = jnp.sqrt(-2.0 * jnp.log(uniform_a)) * jnp.cos(6.283185307179586 * uniform_b)
    return (gauss / math.sqrt(total_columns)).astype(jnp.bfloat16)


def lower_solve(lower, right):
    return lax.linalg.triangular_solve(lower, right, left_side=True, lower=True)


def body(affinity, seed_values, sku_ids):
    col_count = lax.axis_size("col")
    total_columns = sku_ids.shape[0] * col_count
    local_rows = affinity.shape[0]
    piece_rows = local_rows // col_count
    total_rows = local_rows * lax.axis_size("row")
    inv_root = 1.0 / math.sqrt(total_columns)

    def project(left):
        return lax.dot_general(
            left, affinity, (((1,), (1,)), ((), ())), preferred_element_type=jnp.float32
        )

    omega = test_matrix(seed_values, sku_ids, total_columns)
    partial_sketch = project(omega)
    for repeat in range(ITERS + 1):
        sketch = lax.psum(partial_sketch, "col")
        gram = lax.psum(
            jnp.dot(
                sketch,
                sketch.T,
                precision=lax.Precision.HIGHEST,
                preferred_element_type=jnp.float32,
            ),
            "row",
        )
        lower = jnp.linalg.cholesky(gram)
        ortho = lower_solve(lower, sketch)
        if repeat < ITERS:
            back_part = jnp.dot(
                ortho.astype(jnp.bfloat16), affinity, preferred_element_type=jnp.float32
            )
        else:
            start_row = lax.axis_index("col") * piece_rows
            ortho = lax.dynamic_slice_in_dim(ortho, start_row, piece_rows, 1)
        if repeat < ITERS:
            back = lax.psum(back_part, "row")
            partial_sketch = project(back.astype(jnp.bfloat16)) * inv_root
    scale = math.sqrt(total_rows)
    return (ortho * scale, lower.T / scale)


def solution(mesh):
    placed = (P("row", "col"), P(), P("col"))
    return jax.shard_map(
        body, mesh=mesh, in_specs=placed, out_specs=(P(None, ("row", "col")), P()), check_vma=False
    )
```

profile of v0, /device:TPU:0, one launch (start us, length us, event | category | flops | bytes accessed | tf_op | source)
XLA Modules:
  0.0 315.6 jit_solution(10747152659197352157)
XLA Ops:
  7.9 11.5 %fusion.12 = f32[16,4096]{1,0:T(8,128)} fusion(bf16[4096,2048]{1,0:T(8,128)(2,1)} %param.6, s32[2048]{0:T(1024)S(1)} %broadcast_multiply_fusion, s32[16]{0:T(128)} %param.7), kind=kOutput, calls=%fused_computation.22 | convolution fusion | flops 269418496 | bytes 17047616 | tf_op jit(solution)/shard_map/dot_general | solution.py:48
  19.5 35.1 %all-reduce.6.cloned.1.call-done = f32[16,4096]{1,0:T(8,128)} async-done(((f32[16,4096]{1,0:T(8,128)}), f32[16,4096]{1,0:T(8,128)}) %all-reduce.6.cloned.1.call-update) | async-done | bytes 262160 | tf_op jit(solution)/shard_map/psum | solution.py:55
  54.6 1.5 fusion.54
  56.1 21.6 %psum.57 = f32[16,16]{0,1:T(8,128)S(1)} all-reduce(f32[16,16]{0,1:T(8,128)S(1)} %fusion.54), channel_id=1, replica_groups=mesh['row'=8,'col'=4] {'row'}, use_global_device_ids=true, to_apply=%region_1.0 | all-reduce | flops 256 | bytes 2048 | tf_op jit(solution)/shard_map/psum | solution.py:56
  77.8 1.5 cholesky.59
  80.6 1.2 custom-call.7
  81.8 1.4 convolution_convert_fusion.1
  83.2 8.0 %fusion.55 = f32[16,2048]{1,0:T(8,128)S(1)} fusion(bf16[16,4096]{1,0:T(8,128)(2,1)S(1)} %convolution_convert_fusion.1, bf16[4096,2048]{1,0:T(8,128)(2,1)} %param.6), kind=kOutput, calls=%fused_computation.79 | convolution fusion | flops 268435456 | bytes 17039360 | tf_op jit(solution)/shard_map/dot_general | solution.py:68
  91.3 34.2 %all-reduce.11 = bf16[16,2048]{1,0:T(8,128)(2,1)S(1)} all-reduce(f32[16,2048]{1,0:T(8,128)S(1)} %fusion.55), channel_id=1, replica_groups=mesh['row'=8,'col'=4] {'row'}, use_global_device_ids=true, to_apply=%region_4.7 | all-reduce | flops 32768 | bytes 196608 | tf_op jit(solution)/shard_map/psum | solution.py:75
  125.5 10.9 %convolution_multiply_fusion.1 = f32[16,4096]{1,0:T(8,128)} fusion(bf16[4096,2048]{1,0:T(8,128)(2,1)} %param.6, bf16[16,2048]{1,0:T(8,128)(2,1)S(1)} %all-reduce.11), kind=kOutput, calls=%fused_computation.1 | convolution fusion | flops 268500992 | bytes 17104896 | tf_op jit(solution)/shard_map/dot_general | solution.py:48
  136.5 30.3 %all-reduce.8.cloned.1.call-done = f32[16,4096]{1,0:T(8,128)} async-done(((f32[16,4096]{1,0:T(8,128)}), f32[16,4096]{1,0:T(8,128)}) %all-reduce.8.cloned.1.call-update) | async-done | bytes 262160 | tf_op jit(solution)/shard_map/psum | solution.py:55
  166.8 1.5 fusion.56
  168.3 21.8 %psum.60 = f32[16,16]{0,1:T(8,128)S(1)} all-reduce(f32[16,16]{0,1:T(8,128)S(1)} %fusion.56), channel_id=1, replica_groups=mesh['row'=8,'col'=4] {'row'}, use_global_device_ids=true, to_apply=%region_6.9 | all-reduce | flops 256 | bytes 2048 | tf_op jit(solution)/shard_map/psum | solution.py:56
  190.2 1.5 cholesky.70
  192.9 1.2 custom-call.8
  194.2 1.4 convolution_convert_fusion
  195.6 8.0 %fusion.57 = f32[16,2048]{1,0:T(8,128)S(1)} fusion(bf16[16,4096]{1,0:T(8,128)(2,1)S(1)} %convolution_convert_fusion, bf16[4096,2048]{1,0:T(8,128)(2,1)} %param.6), kind=kOutput, calls=%fused_computation.81 | convolution fusion | flops 268435456 | bytes 17039360 | tf_op jit(solution)/shard_map/dot_general | solution.py:68
  203.6 34.2 %all-reduce.12 = bf16[16,2048]{1,0:T(8,128)(2,1)S(1)} all-reduce(f32[16,2048]{1,0:T(8,128)S(1)} %fusion.57), channel_id=1, replica_groups=mesh['row'=8,'col'=4] {'row'}, use_global_device_ids=true, to_apply=%region_7.10 | all-reduce | flops 32768 | bytes 196608 | tf_op jit(solution)/shard_map/psum | solution.py:75
  237.8 10.9 %convolution_multiply_fusion = f32[16,4096]{1,0:T(8,128)} fusion(bf16[4096,2048]{1,0:T(8,128)(2,1)} %param.6, bf16[16,2048]{1,0:T(8,128)(2,1)S(1)} %all-reduce.12), kind=kOutput, calls=%fused_computation | convolution fusion | flops 268500992 | bytes 17104896 | tf_op jit(solution)/shard_map/dot_general | solution.py:48
  248.8 30.4 %all-reduce.10.cloned.1.call-done = f32[16,4096]{1,0:T(8,128)} async-done(((f32[16,4096]{1,0:T(8,128)}), f32[16,4096]{1,0:T(8,128)}) %all-reduce.10.cloned.1.call-update) | async-done | bytes 262160 | tf_op jit(solution)/shard_map/psum | solution.py:55
  279.2 1.5 fusion.58
  280.6 21.6 %psum.63 = f32[16,16]{0,1:T(8,128)S(1)} all-reduce(f32[16,16]{0,1:T(8,128)S(1)} %fusion.58), channel_id=1, replica_groups=mesh['row'=8,'col'=4] {'row'}, use_global_device_ids=true, to_apply=%region_9.12 | all-reduce | flops 256 | bytes 2048 | tf_op jit(solution)/shard_map/psum | solution.py:56
  302.3 1.5 cholesky.81
  307.0 1.4 fusion.31
  (25 shorter events, 7.6 us)
Async XLA Ops:
  7.2 47.5 %all-reduce.6.cloned.1.call-start = ((), (), s32[]{:S(2)}) async-start(), calls=%async_computation | async-start | bytes 524288 | tf_op jit(solution)/shard_map/psum | solution.py:55
  19.5 147.3 %all-reduce.8.cloned.1.call-start = ((), (), s32[]{:S(2)}) async-start(), calls=%async_computation.1 | async-start | bytes 524288 | tf_op jit(solution)/shard_map/psum | solution.py:55
  136.4 142.8 %all-reduce.10.cloned.1.call-start = ((), (), s32[]{:S(2)}) async-start(), calls=%async_computation.2 | async-start | bytes 524288 | tf_op jit(solution)/shard_map/psum | solution.py:55
Sparse Core Ops, SparseCore 0:
  19.6 34.9 all-reduce.5
  136.5 30.2 all-reduce.7
  248.9 30.2 all-reduce.9
where the time goes:
time: 316 us
  blocking collectives  133 us (42%)
  waiting for transfers between devices  95.9 us (30%)
  matrix products  58 us (18%)
  between operations  13.8 us (4%)
  other arithmetic  13.4 us (4%)
    psum x3, waiting for transfers between devices, body(): sketch = lax.psum(partial_sketch, 'col')  95.9 us
    psum x2, blocking collectives, body(): back = lax.psum(back_part, 'row')  68.4 us
    psum x3, blocking collectives, body(): lax.psum(jnp.dot(sketch, sketch.T, precision=lax.Precision.HIGHEST, prefe...  65 us
    dot_general x3, matrix products, project(): lax.dot_general(left, affinity, (((1,), (1,)), ((), ())), preferred_eleme...  33.4 us
    dot_general x2, matrix products, body(): jnp.dot(ortho.astype(jnp.bfloat16), affinity, preferred_element_type=jnp....  16.1 us
    another operation x9, other arithmetic, body(): lower = jnp.linalg.cholesky(gram)  6.39 us
  transfers between devices with their start and end apart: 3, of which 3 were waited for; matrix products, arithmetic and copies ran while one was open for 0% of the time, Pallas kernels for 0%

commit v1 on v0

--- a/solution.py
+++ b/solution.py
@@ -53,14 +53,17 @@
     partial_sketch = project(omega)
     for repeat in range(ITERS + 1):
         sketch = lax.psum(partial_sketch, "col")
-        gram = lax.psum(
-            jnp.dot(
-                sketch,
-                sketch.T,
-                precision=lax.Precision.HIGHEST,
-                preferred_element_type=jnp.float32,
+        gram = jnp.sum(
+            lax.all_gather(
+                jnp.dot(
+                    sketch,
+                    sketch.T,
+                    precision=lax.Precision.HIGHEST,
+                    preferred_element_type=jnp.float32,
+                ),
+                "row",
             ),
-            "row",
+            axis=0,
         )
         lower = jnp.linalg.cholesky(gram)
         ortho = lower_solve(lower, sketch)

time: 316 us -> 348 us (1.10)
  blocking collectives: 133 us -> 169 us
    all_gather x0 -> x3, blocking collectives: none -> 92 us  [body(): lax.all_gather(jnp.dot(sketch, sketch.T, precision=lax.Precision.HIGHEST,...]
    psum x3 -> x0, blocking collectives: 65 us -> none  [body(): lax.psum(jnp.dot(sketch, sketch.T, precision=lax.Precision.HIGHEST, prefe...]
    psum x2, blocking collectives: 68.4 us -> 76.8 us  [body(): back = lax.psum(back_part, 'row')]
where the time goes in v1:
time: 348 us
  blocking collectives  169 us (49%)
  waiting for transfers between devices  92.6 us (27%)
  matrix products  58 us (17%)
  between operations  13.8 us (4%)
  other arithmetic  13.4 us (4%)
    psum x3, waiting for transfers between devices, body(): sketch = lax.psum(partial_sketch, 'col')  92.6 us
    all_gather x3, blocking collectives, body(): lax.all_gather(jnp.dot(sketch, sketch.T, precision=lax.Precision.HIGHEST,...  92 us
    psum x2, blocking collectives, body(): back = lax.psum(back_part, 'row')  76.8 us
    dot_general x3, matrix products, project(): lax.dot_general(left, affinity, (((1,), (1,)), ((), ())), preferred_eleme...  33.4 us
    dot_general x2, matrix products, body(): jnp.dot(ortho.astype(jnp.bfloat16), affinity, preferred_element_type=jnp....  16.1 us
  transfers between devices with their start and end apart: 3, of which 3 were waited for; matrix products, arithmetic and copies ran while one was open for 0% of the time, Pallas kernels for 0%

profile of v1, /device:TPU:0, one launch (start us, length us, event | category | flops | bytes accessed | tf_op | source)
XLA Modules:
  0.0 347.7 jit_solution(17267427875380869731)
XLA Ops:
  7.9 11.5 %fusion.12 = f32[16,4096]{1,0:T(8,128)} fusion(bf16[4096,2048]{1,0:T(8,128)(2,1)} %param.6, s32[2048]{0:T(1024)S(1)} %broadcast_multiply_fusion, s32[16]{0:T(128)} %param.7), kind=kOutput, calls=%fused_computation.22 | convolution fusion | flops 269418496 | bytes 17047616 | tf_op jit(solution)/shard_map/dot_general | solution.py:48
  19.5 35.1 %all-reduce.6.cloned.1.call-done = f32[16,4096]{1,0:T(8,128)} async-done(((f32[16,4096]{1,0:T(8,128)}), f32[16,4096]{1,0:T(8,128)}) %all-reduce.6.cloned.1.call-update) | async-done | bytes 262160 | tf_op jit(solution)/shard_map/psum | solution.py:55
  54.6 1.5 fusion.54
  56.1 30.6 %all-gather = f32[128,16]{1,0:T(8,128)S(1)} all-gather(f32[16,16]{1,0:T(8,128)S(1)} %fusion.54), channel_id=2, replica_groups=mesh['row'=8,'col'=4] {'row'}, dimensions={0}, use_global_device_ids=true | all-gather | bytes 9216 | tf_op jit(solution)/shard_map/all_gather | solution.py:57
  86.8 1.5 cholesky.59
  89.6 1.2 custom-call.7
  90.8 1.4 convolution_convert_fusion.1
  92.2 8.0 %fusion.55 = f32[16,2048]{1,0:T(8,128)S(1)} fusion(bf16[16,4096]{1,0:T(8,128)(2,1)S(1)} %convolution_convert_fusion.1, bf16[4096,2048]{1,0:T(8,128)(2,1)} %param.6), kind=kOutput, calls=%fused_computation.79 | convolution fusion | flops 268435456 | bytes 17039360 | tf_op jit(solution)/shard_map/dot_general | solution.py:71
  100.3 38.4 %all-reduce.11 = bf16[16,2048]{1,0:T(8,128)(2,1)S(1)} all-reduce(f32[16,2048]{1,0:T(8,128)S(1)} %fusion.55), channel_id=1, replica_groups=mesh['row'=8,'col'=4] {'row'}, use_global_device_ids=true, to_apply=%region_4.7 | all-reduce | flops 32768 | bytes 196608 | tf_op jit(solution)/shard_map/psum | solution.py:78
  138.7 10.9 %convolution_multiply_fusion.1 = f32[16,4096]{1,0:T(8,128)} fusion(bf16[4096,2048]{1,0:T(8,128)(2,1)} %param.6, bf16[16,2048]{1,0:T(8,128)(2,1)S(1)} %all-reduce.11), kind=kOutput, calls=%fused_computation.1 | convolution fusion | flops 268500992 | bytes 17104896 | tf_op jit(solution)/shard_map/dot_general | solution.py:48
  149.7 28.7 %all-reduce.8.cloned.1.call-done = f32[16,4096]{1,0:T(8,128)} async-done(((f32[16,4096]{1,0:T(8,128)}), f32[16,4096]{1,0:T(8,128)}) %all-reduce.8.cloned.1.call-update) | async-done | bytes 262160 | tf_op jit(solution)/shard_map/psum | solution.py:55
  178.4 1.5 fusion.56
  179.8 30.8 %all-gather.1 = f32[128,16]{1,0:T(8,128)S(1)} all-gather(f32[16,16]{1,0:T(8,128)S(1)} %fusion.56), channel_id=3, replica_groups=mesh['row'=8,'col'=4] {'row'}, dimensions={0}, use_global_device_ids=true | all-gather | bytes 9216 | tf_op jit(solution)/shard_map/all_gather | solution.py:57
  210.7 1.5 cholesky.70
  213.5 1.2 custom-call.8
  214.8 1.4 convolution_convert_fusion
  216.1 8.0 %fusion.57 = f32[16,2048]{1,0:T(8,128)S(1)} fusion(bf16[16,4096]{1,0:T(8,128)(2,1)S(1)} %convolution_convert_fusion, bf16[4096,2048]{1,0:T(8,128)(2,1)} %param.6), kind=kOutput, calls=%fused_computation.81 | convolution fusion | flops 268435456 | bytes 17039360 | tf_op jit(solution)/shard_map/dot_general | solution.py:71
  224.2 38.4 %all-reduce.12 = bf16[16,2048]{1,0:T(8,128)(2,1)S(1)} all-reduce(f32[16,2048]{1,0:T(8,128)S(1)} %fusion.57), channel_id=1, replica_groups=mesh['row'=8,'col'=4] {'row'}, use_global_device_ids=true, to_apply=%region_7.10 | all-reduce | flops 32768 | bytes 196608 | tf_op jit(solution)/shard_map/psum | solution.py:78
  262.6 10.9 %convolution_multiply_fusion = f32[16,4096]{1,0:T(8,128)} fusion(bf16[4096,2048]{1,0:T(8,128)(2,1)} %param.6, bf16[16,2048]{1,0:T(8,128)(2,1)S(1)} %all-reduce.12), kind=kOutput, calls=%fused_computation | convolution fusion | flops 268500992 | bytes 17104896 | tf_op jit(solution)/shard_map/dot_general | solution.py:48
  273.5 28.7 %all-reduce.10.cloned.1.call-done = f32[16,4096]{1,0:T(8,128)} async-done(((f32[16,4096]{1,0:T(8,128)}), f32[16,4096]{1,0:T(8,128)}) %all-reduce.10.cloned.1.call-update) | async-done | bytes 262160 | tf_op jit(solution)/shard_map/psum | solution.py:55
  302.3 1.5 fusion.58
  303.8 30.6 %all-gather.2 = f32[128,16]{1,0:T(8,128)S(1)} all-gather(f32[16,16]{1,0:T(8,128)S(1)} %fusion.58), channel_id=4, replica_groups=mesh['row'=8,'col'=4] {'row'}, dimensions={0}, use_global_device_ids=true | all-gather | bytes 9216 | tf_op jit(solution)/shard_map/all_gather | solution.py:57
  334.5 1.5 cholesky.81
  339.2 1.4 fusion.31
  (28 shorter events, 7.7 us)
Async XLA Ops:
  7.2 47.5 %all-reduce.6.cloned.1.call-start = ((), (), s32[]{:S(2)}) async-start(), calls=%async_computation | async-start | bytes 524288 | tf_op jit(solution)/shard_map/psum | solution.py:55
  19.5 158.9 %all-reduce.8.cloned.1.call-start = ((), (), s32[]{:S(2)}) async-start(), calls=%async_computation.1 | async-start | bytes 524288 | tf_op jit(solution)/shard_map/psum | solution.py:55
  149.6 152.7 %all-reduce.10.cloned.1.call-start = ((), (), s32[]{:S(2)}) async-start(), calls=%async_computation.2 | async-start | bytes 524288 | tf_op jit(solution)/shard_map/psum | solution.py:55
Sparse Core Ops, SparseCore 0:
  19.6 34.9 all-reduce.5
  149.7 28.5 all-reduce.7
  273.7 28.5 all-reduce.9
